TPU v7x, 32 devices: a whole 2x2x4 slice. The times are simulated.
32 devices in a mesh: dp: 2 (over x), fsdp: 16 (over z, y, core).
Axes of the slice: x: 2, y: 2, z: 4, core: 2. Of those that a mesh axis runs over, the one named last changes fastest.
Arguments:
- tokens: bfloat16 [32, 512, 768], P(('dp', 'fsdp')), may hold values from -6 to 6
- cotangent: bfloat16 [32, 512, 768], P(('dp', 'fsdp')), may hold values from -6 to 6
- time_embed: bfloat16 [32, 768], P(('dp', 'fsdp')), may hold values from -3 to 3
- cath_class: int32 [32], P(('dp', 'fsdp')), may hold values from 0 to 4
- cath_arch: int32 [32], P(('dp', 'fsdp')), may hold values from 0 to 42
- cath_topo: int32 [32], P(('dp', 'fsdp')), may hold values from 0 to 1471
- res_counts: int32 [32], P(('dp', 'fsdp')), may hold values from 256 to 512, as said below
- chain_ids: int32 [32, 512], P(('dp', 'fsdp')), may hold values from 0 to 1, as said below
- break_mask: int32 [32, 512], P(('dp', 'fsdp')), may hold values from 0 to 1, as said below
- w_ada: bfloat16 [768, 4608], P('fsdp'), may hold values from -0.21875 to 0.21875
- w_qkv: bfloat16 [768, 2304], P('fsdp'), may hold values from -0.21875 to 0.21875
- w_out: bfloat16 [768, 768], P('fsdp'), may hold values from -1.5 to 1.5
- w_gate: bfloat16 [768, 3072], P('fsdp'), may hold values from -0.21875 to 0.21875
- w_up: bfloat16 [768, 3072], P('fsdp'), may hold values from -0.21875 to 0.21875
- w_down: bfloat16 [3072, 768], P(None, 'fsdp'), may hold values from -0.21875 to 0.21875
- table_class: bfloat16 [5, 768], P(None, 'fsdp'), may hold values from -3 to 3
- table_arch: bfloat16 [43, 768], P(None, 'fsdp'), may hold values from -3 to 3
- table_topo: bfloat16 [1472, 768], P(None, 'fsdp'), may hold values from -3 to 3
- break_vec: bfloat16 [768], P('fsdp'), may hold values from -4 to 4
- pair_table: bfloat16 [128, 256], P(None, 'fsdp'), may hold values from -5 to 5
- pair_proj: bfloat16 [256, 12], P('fsdp'), may hold values from -0.375 to 0.375
Outputs:
- output: bfloat16 [32, 512, 768], P(('dp', 'fsdp'))
- d_tokens: bfloat16 [32, 512, 768], P(('dp', 'fsdp'))
- grad_ada: float32 [768, 4608], P('fsdp')
- grad_qkv: float32 [768, 2304], P('fsdp')
- grad_out: float32 [768, 768], P('fsdp')
- grad_gate: float32 [768, 3072], P('fsdp')
- grad_up: float32 [768, 3072], P('fsdp')
- grad_down: float32 [3072, 768], P(None, 'fsdp')
- grad_class: float32 [5, 768], P(None, 'fsdp')
- grad_arch: float32 [43, 768], P(None, 'fsdp')
- grad_topo: float32 [1472, 768], P(None, 'fsdp')
- grad_break: float32 [768], P('fsdp')
- grad_pair: float32 [128, 256], P(None, 'fsdp')
- grad_proj: float32 [256, 12], P('fsdp')
Inputs may be any that keep to these rules, and one draw needn't show every extreme that they name: `res_counts`: keys at or past a window's count are padding. `chain_ids`: 0 up to a window's second chain, 1 from it on; never falls along a window. `break_mask`: 1 at the first residue of a window's second chain and after gaps in a crop, else 0; slot 0 is never marked.
All inputs are finite; a program needn't handle non-finite values.
Results may differ from a plain program's by a relative error of at most 0.015.
Values may be sent and summed in bfloat16 or wider, within the bound.
A program may use at most 256 MiB of HBM per device.

v0:
```python
from functools import partial

import jax
import jax.numpy as jnp
from jax import lax
from jax.experimental import pallas as pl
from jax.experimental.pallas import tpu as pltpu
from jax.sharding import PartitionSpec as P

epsilon = 1e-05
highest = lax.Precision.HIGHEST


def matmul(left, right):
    return jnp.dot(left, right, preferred_element_type=jnp.float32)


def matmul_t(left, right):
    return lax.dot_general(
        left, right, (((1,), (1,)), ((), ())), preferred_element_type=jnp.float32
    )


def matmul_tn(left, right):
    return lax.dot_general(
        left, right, (((0,), (0,)), ((), ())), preferred_element_type=jnp.float32
    )


def exact_tn(left, right):
    return lax.dot_general(
        left, right, (((0,), (0,)), ((), ())), precision=highest, preferred_element_type=jnp.float32
    )


def exact_nt(left, right):
    return lax.dot_general(
        left, right, (((1,), (1,)), ((), ())), precision=highest, preferred_element_type=jnp.float32
    )


def normalize(values):
    centred = values - jnp.mean(values, axis=-1, keepdims=True)
    inv_std = lax.rsqrt(jnp.mean(centred * centred, axis=-1, keepdims=True) + epsilon)
    return (centred * inv_std, inv_std)


def normalize_back(normed, inv_std, grad):
    return inv_std * (
        grad
        - jnp.mean(grad, axis=-1, keepdims=True)
        - normed * jnp.mean(grad * normed, axis=-1, keepdims=True)
    )


def pair_classes(chain_row, class_count):
    length = chain_row.shape[0]
    position = jnp.arange(length, dtype=jnp.int32)
    reach = class_count // 2 - 1
    offset = jnp.clip(position[:, None] - position[None, :], -reach, reach) + reach
    return jnp.where(chain_row[:, None] == chain_row[None, :], offset, class_count - 1)


def pair_bias(classes, bias_table):
    length = classes.shape[0]
    step_rows = min(length, 128)
    class_ids = jnp.arange(bias_table.shape[0], dtype=jnp.int32)

    def one_block(row_block):
        onehot = (row_block[:, :, None] == class_ids).astype(jnp.bfloat16)
        return jnp.einsum("ijc,ch->hij", onehot, bias_table, preferred_element_type=jnp.float32)

    pieces = lax.map(one_block, classes.reshape(length // step_rows, step_rows, length))
    return jnp.transpose(pieces, (1, 0, 2, 3)).reshape(bias_table.shape[1], length, length)


def pair_bias_back(classes, d_scores, class_count):
    head_count, length = (d_scores.shape[0], d_scores.shape[1])
    step_rows = min(length, 128)
    block_count = length // step_rows
    class_ids = jnp.arange(class_count, dtype=jnp.int32)
    grad_blocks = jnp.transpose(
        d_scores.reshape(head_count, block_count, step_rows, length), (1, 0, 2, 3)
    )

    def add_block(running, inputs):
        row_block, grad_block = inputs
        onehot = (row_block[:, :, None] == class_ids).astype(jnp.bfloat16)
        return (
            running
            + jnp.einsum("hij,ijc->ch", grad_block, onehot, preferred_element_type=jnp.float32),
            None,
        )

    start = jnp.zeros((class_count, head_count), jnp.float32)
    summed, unused = lax.scan(
        add_block, start, (classes.reshape(block_count, step_rows, length), grad_blocks)
    )
    return summed


def split_heads(qkv_win, head_count):
    length, triple = qkv_win.shape
    shaped = qkv_win.reshape(length, 3, head_count, triple // (3 * head_count))
    return (shaped[:, 0], shaped[:, 1], shaped[:, 2])


def window_scores(qkv_win, chain_row, count_win, bias_table):
    length = qkv_win.shape[0]
    queries, key_rows, value_rows = split_heads(qkv_win, bias_table.shape[1])
    classes = pair_classes(chain_row, bias_table.shape[0])
    score_scale = queries.shape[-1] ** (-0.5)
    scores = (
        jnp.einsum("qhd,khd->hqk", queries, key_rows, preferred_element_type=jnp.float32)
        * score_scale
    )
    scores = scores + pair_bias(classes, bias_table)
    live_keys = jnp.arange(length, dtype=jnp.int32) < count_win
    scores = jnp.where(live_keys[None, None, :], scores, -1e30)
    return (scores, queries, key_rows, value_rows, classes, score_scale)


def attend(inputs, bias_table):
    qkv_win, chain_row, count_win = inputs
    scores, queries, key_rows, value_rows, classes, score_scale = window_scores(
        qkv_win, chain_row, count_win, bias_table
    )
    highest_score = jnp.max(scores, axis=-1, keepdims=True)
    exponent = jnp.exp(scores - highest_score)
    row_total = jnp.sum(exponent, axis=-1, keepdims=True)
    attn_probs = (exponent / row_total).astype(jnp.bfloat16)
    attended = jnp.einsum(
        "hqk,khd->qhd", attn_probs, value_rows, preferred_element_type=jnp.float32
    )
    attended = attended.reshape(qkv_win.shape[0], -1).astype(jnp.bfloat16)
    return (attended, (highest_score + jnp.log(row_total))[:, :, 0])


def attend_back(inputs, bias_table):
    qkv_win, chain_row, count_win, log_total, d_attended = inputs
    scores, queries, key_rows, value_rows, classes, score_scale = window_scores(
        qkv_win, chain_row, count_win, bias_table
    )
    attn_probs = jnp.exp(scores - log_total[:, :, None])
    d_heads = d_attended.reshape(queries.shape)
    d_probs = jnp.einsum("qhd,khd->hqk", d_heads, value_rows, preferred_element_type=jnp.float32)
    d_scores = attn_probs * (d_probs - jnp.sum(attn_probs * d_probs, axis=-1, keepdims=True))
    d_scores = d_scores.astype(jnp.bfloat16)
    d_values = jnp.einsum(
        "hqk,qhd->khd", attn_probs.astype(jnp.bfloat16), d_heads, preferred_element_type=jnp.float32
    )
    d_queries = (
        jnp.einsum("hqk,khd->qhd", d_scores, key_rows, preferred_element_type=jnp.float32)
        * score_scale
    )
    d_keys = (
        jnp.einsum("hqk,qhd->khd", d_scores, queries, preferred_element_type=jnp.float32)
        * score_scale
    )
    d_qkv = (
        jnp.stack([d_queries, d_keys, d_values], axis=1)
        .reshape(qkv_win.shape[0], -1)
        .astype(jnp.bfloat16)
    )
    return (d_qkv, pair_bias_back(classes, d_scores, bias_table.shape[0]))


def forward(
    tokens,
    time_embed,
    cath_class,
    cath_arch,
    cath_topo,
    res_counts,
    chain_ids,
    break_mask,
    attn_set,
    mlp_set,
):
    ada_all, qkv_all, out_all, class_all, arch_all, topo_all, break_all, pair_all, proj_all = (
        attn_set
    )
    gate_all, up_all, down_all = mlp_set
    windows, length, model_width = tokens.shape
    row_count = windows * length
    pre_act = time_embed.astype(jnp.float32)
    onehots = []
    for labels, lookup in ((cath_class, class_all), (cath_arch, arch_all), (cath_topo, topo_all)):
        onehot = (labels[:, None] == jnp.arange(lookup.shape[0], dtype=jnp.int32)[None, :]).astype(
            jnp.bfloat16
        )
        pre_act = pre_act + matmul(onehot, lookup)
        onehots.append(onehot)
    cond_low = jax.nn.silu(pre_act).astype(jnp.bfloat16)
    ada_rows = matmul(cond_low, ada_all)
    shift_one, scale_one, gate_one, shift_two, scale_two, gate_two = [
        portion[:, None, :] for portion in jnp.split(ada_rows, 6, axis=1)
    ]
    resid_in = tokens.astype(jnp.float32)
    normed_one, inv_one = normalize(resid_in)
    break_rows = break_mask.astype(jnp.float32)[:, :, None]
    h_one_low = (
        normed_one * (1.0 + scale_one) + shift_one + break_rows * break_all.astype(jnp.float32)
    )
    h_one_low = h_one_low.astype(jnp.bfloat16).reshape(row_count, model_width)
    proj_qkv = (
        matmul(h_one_low, qkv_all).astype(jnp.bfloat16).reshape(windows, length, 3 * model_width)
    )
    pair_normed, pair_inv = normalize(pair_all.astype(jnp.float32))
    pair_low = pair_normed.astype(jnp.bfloat16)
    bias_table = matmul(pair_low, proj_all).astype(jnp.bfloat16)
    attended, log_total = lax.map(
        partial(attend, bias_table=bias_table), (proj_qkv, chain_ids, res_counts)
    )
    attended_rows = attended.reshape(row_count, model_width)
    attn_proj = matmul(attended_rows, out_all).reshape(windows, length, model_width)
    middle = resid_in + gate_one * attn_proj
    normed_two, inv_two = normalize(middle)
    h_two_low = (
        (normed_two * (1.0 + scale_two) + shift_two)
        .astype(jnp.bfloat16)
        .reshape(row_count, model_width)
    )
    gate_pre = matmul(h_two_low, gate_all)
    up_pre = matmul(h_two_low, up_all)
    activated = (jax.nn.silu(gate_pre) * up_pre).astype(jnp.bfloat16)
    ffn_out = matmul(activated, down_all).reshape(windows, length, model_width)
    output = middle + gate_two * ffn_out
    return {
        "output": output,
        "pre_act": pre_act,
        "onehots": onehots,
        "cond_low": cond_low,
        "scales": (scale_one, gate_one, scale_two, gate_two),
        "normed_one": normed_one,
        "inv_one": inv_one,
        "break_rows": break_rows,
        "h_one_low": h_one_low,
        "proj_qkv": proj_qkv,
        "pair_normed": pair_normed,
        "pair_inv": pair_inv,
        "pair_low": pair_low,
        "bias_table": bias_table,
        "log_total": log_total,
        "attended_rows": attended_rows,
        "attn_proj": attn_proj,
        "normed_two": normed_two,
        "inv_two": inv_two,
        "h_two_low": h_two_low,
        "gate_pre": gate_pre,
        "up_pre": up_pre,
        "activated": activated,
        "ffn_out": ffn_out,
    }


def shards(
    tokens,
    cotangent,
    time_embed,
    cath_class,
    cath_arch,
    cath_topo,
    res_counts,
    chain_ids,
    break_mask,
    w_ada,
    w_qkv,
    w_out,
    w_gate,
    w_up,
    w_down,
    table_class,
    table_arch,
    table_topo,
    break_vec,
    pair_table,
    pair_proj,
):
    attn_set = (
        lax.all_gather(w_ada, "fsdp", axis=0, tiled=True),
        lax.all_gather(w_qkv, "fsdp", axis=0, tiled=True),
        lax.all_gather(w_out, "fsdp", axis=0, tiled=True),
        lax.all_gather(table_class, "fsdp", axis=1, tiled=True),
        lax.all_gather(table_arch, "fsdp", axis=1, tiled=True),
        lax.all_gather(table_topo, "fsdp", axis=1, tiled=True),
        lax.all_gather(break_vec, "fsdp", axis=0, tiled=True),
        lax.all_gather(pair_table, "fsdp", axis=1, tiled=True),
        lax.all_gather(pair_proj, "fsdp", axis=0, tiled=True),
    )
    mlp_set = (
        lax.all_gather(w_gate, "fsdp", axis=0, tiled=True),
        lax.all_gather(w_up, "fsdp", axis=0, tiled=True),
        lax.all_gather(w_down, "fsdp", axis=1, tiled=True),
    )
    saved = forward(
        tokens,
        time_embed,
        cath_class,
        cath_arch,
        cath_topo,
        res_counts,
        chain_ids,
        break_mask,
        attn_set,
        mlp_set,
    )
    output = saved["output"].astype(jnp.bfloat16)
    attn_set = (
        lax.all_gather(w_ada, "fsdp", axis=0, tiled=True),
        lax.all_gather(w_qkv, "fsdp", axis=0, tiled=True),
        lax.all_gather(w_out, "fsdp", axis=0, tiled=True),
        lax.all_gather(table_class, "fsdp", axis=1, tiled=True),
        lax.all_gather(table_arch, "fsdp", axis=1, tiled=True),
        lax.all_gather(table_topo, "fsdp", axis=1, tiled=True),
        lax.all_gather(break_vec, "fsdp", axis=0, tiled=True),
        lax.all_gather(pair_table, "fsdp", axis=1, tiled=True),
        lax.all_gather(pair_proj, "fsdp", axis=0, tiled=True),
    )
    mlp_set = (
        lax.all_gather(w_gate, "fsdp", axis=0, tiled=True),
        lax.all_gather(w_up, "fsdp", axis=0, tiled=True),
        lax.all_gather(w_down, "fsdp", axis=1, tiled=True),
    )
    saved = forward(
        tokens,
        time_embed,
        cath_class,
        cath_arch,
        cath_topo,
        res_counts,
        chain_ids,
        break_mask,
        attn_set,
        mlp_set,
    )
    ada_all, qkv_all, out_all, class_all, arch_all, topo_all, break_all, pair_all, proj_all = (
        attn_set
    )
    gate_all, up_all, down_all = mlp_set
    windows, length, model_width = tokens.shape
    row_count = windows * length
    scale_one, gate_one, scale_two, gate_two = saved["scales"]
    grad_rows = cotangent.astype(jnp.float32)
    ffn_out = saved["ffn_out"]
    d_ffn = (gate_two * grad_rows).astype(jnp.bfloat16).reshape(row_count, model_width)
    d_gate_two = jnp.sum(grad_rows * ffn_out, axis=1)
    grad_down = matmul_tn(saved["activated"], d_ffn)
    d_act = matmul_t(d_ffn, down_all)
    gate_pre, up_pre = (saved["gate_pre"], saved["up_pre"])
    sigma = jax.nn.sigmoid(gate_pre)
    d_gate_pre = (d_act * up_pre * sigma * (1.0 + gate_pre * (1.0 - sigma))).astype(jnp.bfloat16)
    d_up_pre = (d_act * gate_pre * sigma).astype(jnp.bfloat16)
    h_two_low = saved["h_two_low"]
    grad_gate = matmul_tn(h_two_low, d_gate_pre)
    grad_up = matmul_tn(h_two_low, d_up_pre)
    d_h_two = (matmul_t(d_gate_pre, gate_all) + matmul_t(d_up_pre, up_all)).reshape(
        windows, length, model_width
    )
    normed_two = saved["normed_two"]
    d_scale_two = jnp.sum(d_h_two * normed_two, axis=1)
    d_shift_two = jnp.sum(d_h_two, axis=1)
    d_middle = grad_rows + normalize_back(normed_two, saved["inv_two"], d_h_two * (1.0 + scale_two))
    d_gate_one = jnp.sum(d_middle * saved["attn_proj"], axis=1)
    d_attn = (gate_one * d_middle).astype(jnp.bfloat16).reshape(row_count, model_width)
    grad_out = matmul_tn(saved["attended_rows"], d_attn)
    d_attended = (
        matmul_t(d_attn, out_all).astype(jnp.bfloat16).reshape(windows, length, model_width)
    )
    bias_table = saved["bias_table"]
    d_qkv, bias_grads = lax.map(
        partial(attend_back, bias_table=bias_table),
        (saved["proj_qkv"], chain_ids, res_counts, saved["log_total"], d_attended),
    )
    d_bias_table = jnp.sum(bias_grads, axis=0)
    d_qkv = d_qkv.reshape(row_count, 3 * model_width)
    h_one_low = saved["h_one_low"]
    grad_qkv = matmul_tn(h_one_low, d_qkv)
    d_h_one = matmul_t(d_qkv, qkv_all).reshape(windows, length, model_width)
    normed_one = saved["normed_one"]
    d_scale_one = jnp.sum(d_h_one * normed_one, axis=1)
    d_shift_one = jnp.sum(d_h_one, axis=1)
    grad_break = jnp.sum(d_h_one * saved["break_rows"], axis=(0, 1))
    d_tokens = d_middle + normalize_back(normed_one, saved["inv_one"], d_h_one * (1.0 + scale_one))
    d_ada = jnp.concatenate(
        [d_shift_one, d_scale_one, d_gate_one, d_shift_two, d_scale_two, d_gate_two], axis=1
    ).astype(jnp.bfloat16)
    grad_ada = matmul_tn(saved["cond_low"], d_ada)
    pre_act = saved["pre_act"]
    sigma_pre = jax.nn.sigmoid(pre_act)
    d_pre = matmul_t(d_ada, ada_all) * sigma_pre * (1.0 + pre_act * (1.0 - sigma_pre))
    onehots = saved["onehots"]
    grad_class = exact_tn(onehots[0].astype(jnp.float32), d_pre)
    grad_arch = exact_tn(onehots[1].astype(jnp.float32), d_pre)
    grad_topo = exact_tn(onehots[2].astype(jnp.float32), d_pre)
    grad_proj = exact_tn(saved["pair_low"].astype(jnp.float32), d_bias_table)
    d_pair_normed = exact_nt(d_bias_table, proj_all.astype(jnp.float32))
    grad_pair = normalize_back(saved["pair_normed"], saved["pair_inv"], d_pair_normed)
    attn_parts = (
        lax.psum_scatter(grad_ada, "fsdp", scatter_dimension=0, tiled=True),
        lax.psum_scatter(grad_qkv, "fsdp", scatter_dimension=0, tiled=True),
        lax.psum_scatter(grad_out, "fsdp", scatter_dimension=0, tiled=True),
        lax.psum_scatter(grad_class, "fsdp", scatter_dimension=1, tiled=True),
        lax.psum_scatter(grad_arch, "fsdp", scatter_dimension=1, tiled=True),
        lax.psum_scatter(grad_topo, "fsdp", scatter_dimension=1, tiled=True),
        lax.psum_scatter(grad_break, "fsdp", scatter_dimension=0, tiled=True),
        lax.psum_scatter(grad_pair, "fsdp", scatter_dimension=1, tiled=True),
        lax.psum_scatter(grad_proj, "fsdp", scatter_dimension=0, tiled=True),
    )
    mlp_parts = (
        lax.psum_scatter(grad_gate, "fsdp", scatter_dimension=0, tiled=True),
        lax.psum_scatter(grad_up, "fsdp", scatter_dimension=0, tiled=True),
        lax.psum_scatter(grad_down, "fsdp", scatter_dimension=1, tiled=True),
    )
    owned = (
        lax.psum(attn_parts[0].astype(jnp.bfloat16), "dp").astype(jnp.float32),
        lax.psum(attn_parts[1].astype(jnp.bfloat16), "dp").astype(jnp.float32),
        lax.psum(attn_parts[2].astype(jnp.bfloat16), "dp").astype(jnp.float32),
        lax.psum(mlp_parts[0].astype(jnp.bfloat16), "dp").astype(jnp.float32),
        lax.psum(mlp_parts[1].astype(jnp.bfloat16), "dp").astype(jnp.float32),
        lax.psum(mlp_parts[2].astype(jnp.bfloat16), "dp").astype(jnp.float32),
        lax.psum(attn_parts[3].astype(jnp.bfloat16), "dp").astype(jnp.float32),
        lax.psum(attn_parts[4].astype(jnp.bfloat16), "dp").astype(jnp.float32),
        lax.psum(attn_parts[5].astype(jnp.bfloat16), "dp").astype(jnp.float32),
        lax.psum(attn_parts[6].astype(jnp.bfloat16), "dp").astype(jnp.float32),
        lax.psum(attn_parts[7].astype(jnp.bfloat16), "dp").astype(jnp.float32),
        lax.psum(attn_parts[8].astype(jnp.bfloat16), "dp").astype(jnp.float32),
    )
    return (
        output,
        d_tokens.astype(jnp.bfloat16),
        owned[0],
        owned[1],
        owned[2],
        owned[3],
        owned[4],
        owned[5],
        owned[6],
        owned[7],
        owned[8],
        owned[9],
        owned[10],
        owned[11],
    )


mesh_ids = pl.DeviceIdType.MESH
f32 = jnp.float32
b16 = jnp.bfloat16
core_count = 2
chip_count = 8
shard_rows = 48
chunk_cols = 3072
chunk_count = 4
side_cols = 768
ring_cols = 2304
job_cols = 384
jobs_in_chunk = 6
job_count = 24
ahead = 3
gather_stride = 2
scatter_stride = 2
grad_buffers = 3
plan = (1, 1, 1, 1, 1, 1, 1, 1, 1, 1, 5)
ahead_plan = (2, 2, 2, 2, 2)


def dot_nn(left, right):
    return jnp.dot(left, right, preferred_element_type=f32)


def dot_nt(left, right):
    return lax.dot_general(left, right, (((1,), (1,)), ((), ())), preferred_element_type=f32)


def dot_tn(left, right):
    return lax.dot_general(left, right, (((0,), (0,)), ((), ())), preferred_element_type=f32)


def on(condition, body):
    if isinstance(condition, bool):
        if condition:
            body()
    else:
        pl.when(condition)(body)


def both(first, second):
    if isinstance(first, bool) and isinstance(second, bool):
        return first and second
    return jnp.logical_and(first, second)


def quot(value, by):
    return value // by if isinstance(value, int) else lax.div(value, by)


def modulo(value, by):
    return value % by if isinstance(value, int) else lax.rem(value, by)


def aligned(value, by=128):
    return value if isinstance(value, int) else pl.multiple_of(value, by)


class Place:
    def __init__(self):
        self.x = lax.axis_index("dp")
        self.f = lax.axis_index("fsdp")
        self.me = self.x * 16 + self.f
        self.c = lax.rem(self.f, 2)
        self.cy = lax.div(self.f, 2)
        y = lax.rem(self.cy, 2)
        z = lax.div(self.cy, 2)
        self.p = z * (1 - y) + (7 - z) * y

    def chip(self, position):
        position = lax.rem(position + 16, 8)
        half = lax.div(position, 4)
        return 2 * position * (1 - half) + (15 - 2 * position) * half

    def ring_id(self, position):
        return (self.x, self.chip(position) * 2 + self.c)

    def plane_id(self):
        return (1 - self.x, self.f)

    def core_id(self):
        return (self.x, self.cy * 2 + 1 - self.c)


def greet_all(at):
    barrier = pltpu.get_barrier_semaphore()

    @pl.loop(1, 32)
    def _(step):
        other = lax.rem(at.me + step, 32)
        pl.semaphore_signal(
            barrier,
            inc=1,
            device_id=(lax.div(other, 16), lax.rem(other, 16)),
            device_id_type=mesh_ids,
        )

    pl.semaphore_wait(barrier, 31)


def remote(src, dst, send_sem, recv_sem, device_id):
    return pltpu.make_async_remote_copy(
        src_ref=src,
        dst_ref=dst,
        send_sem=send_sem,
        recv_sem=recv_sem,
        device_id=device_id,
        device_id_type=mesh_ids,
    )


def job_column(at, job):
    chunk = quot(job, jobs_in_chunk)
    inner = modulo(job, jobs_in_chunk)
    base = chunk * chunk_cols + inner * job_cols
    if isinstance(job, int):
        return aligned(base + (at.x * ring_cols if inner < 2 else 0))
    side = 1 - jnp.minimum(lax.div(inner, 2), 1)
    return aligned(base + side * at.x * ring_cols)


class Gather:
    def __init__(self, at, packed, held, sems):
        self.at = at
        self.packed = packed
        self.held = held
        (
            self.ring_send,
            self.ring_recv,
            self.side_send,
            self.side_recv,
            self.core_send,
            self.core_recv,
        ) = sems

    def ring(self, job, step, way, hop):
        at = self.at
        sign = 1 - 2 * way
        column = pl.ds(job_column(at, job), job_cols)
        block = self.held.at[at.chip(at.p - (step + hop) * sign), at.c, :, column]
        src = self.packed.at[:, column] if step == 0 and hop == 0 else block
        return remote(
            src,
            block,
            self.ring_send.at[job, step, way],
            self.ring_recv.at[job, step, way],
            at.ring_id(at.p + sign),
        )

    def relay(self, job, step, way):
        at = self.at
        sign = 1 - 2 * way
        column = pl.ds(job_column(at, job), job_cols)
        block = self.held.at[at.chip(at.p - (step + 1) * sign), at.c, :, column]
        self.pass_on(block, block, job)

    def pass_on(self, src, dst, job):
        at = self.at
        chunk = quot(job, jobs_in_chunk)
        inner = modulo(job, jobs_in_chunk)
        slot = chunk * 2
        remote(
            src, dst, self.core_send.at[slot], self.core_recv.at[slot], at.core_id()
        ).start()

        def across():
            spot = chunk * 2 + inner
            remote(
                src, dst, self.side_send.at[spot], self.side_recv.at[spot], at.plane_id()
            ).start()

        on(inner < 2, across)

    def side(self, job, mine):
        at = self.at
        chunk = quot(job, jobs_in_chunk)
        inner = modulo(job, jobs_in_chunk)
        owner = at.x if mine else 1 - at.x
        column = aligned(chunk * chunk_cols + inner * job_cols + owner * ring_cols)
        block = self.held.at[:, at.c, :, pl.ds(column, job_cols)]
        slot = chunk * 2 + inner
        return remote(
            block, block, self.side_send.at[slot], self.side_recv.at[slot], at.plane_id()
        )

    def core(self, chunk, part, mine):
        at = self.at
        if part == 0:
            column, width = chunk * chunk_cols + at.x * side_cols, ring_cols
        else:
            column, width = chunk * chunk_cols + (1 - at.x) * ring_cols, side_cols
        row = at.c if mine else 1 - at.c
        block = self.held.at[:, row, :, pl.ds(aligned(column), width)]
        slot = chunk * 2 + part
        return remote(block, block, self.core_send.at[slot], self.core_recv.at[slot], at.core_id())

    def start(self, job):
        self.ring(job, 0, 0, 0).start()
        self.ring(job, 0, 1, 0).start()
        at = self.at
        column = pl.ds(job_column(at, job), job_cols)
        self.pass_on(self.packed.at[:, column], self.held.at[at.cy, at.c, :, column], job)

    def tick(self, tau):
        def valid(job):
            return both(job >= 0, job < job_count)

        for step in (4, 3, 2, 1):
            job = tau - step * gather_stride

            def advance(job=job, step=step):
                if step < 4:
                    ways = (0, 1)
                else:
                    ways = (modulo(job, 2),)
                for way in ways:
                    self.ring(job, step - 1, way, 1).wait_recv()
                if step < 3:
                    self.ring(job, step, 0, 0).start()
                    self.ring(job, step, 1, 0).start()
                elif step == 3:
                    self.ring(job, 3, modulo(job, 2), 0).start()
                for way in ways:
                    self.relay(job, step - 1, way)

            on(valid(job), advance)
        on(valid(tau + ahead), lambda: self.start(tau + ahead))

        late = tau - 4 * gather_stride - jobs_in_chunk

        def side_done():
            chunk = quot(late, jobs_in_chunk)
            self.side(chunk * jobs_in_chunk, False).wait_recv()
            self.side(chunk * jobs_in_chunk + 1, False).wait_recv()
            self.core(chunk, 1, True).start()

        on(both(valid(late), modulo(late + 60, jobs_in_chunk) == 0), side_done)

    def arrive(self, chunk):
        self.core(chunk, 0, False).wait_recv()
        self.core(chunk, 1, False).wait_recv()

    def finish(self):
        @pl.loop(0, job_count)
        def _(job):
            for step in range(3):
                self.ring(job, step, 0, 0).wait_send()
                self.ring(job, step, 1, 0).wait_send()
            self.ring(job, 3, lax.rem(job, 2), 0).wait_send()

        for chunk in range(chunk_count):
            for inner in range(2):
                self.side(chunk * jobs_in_chunk + inner, True).wait_send()
                self.core(chunk, inner, True).wait_send()


def class_map(class_count):
    spot = lax.broadcasted_iota(jnp.int32, (512, class_count), 0)
    spot = jnp.where(spot < 384, spot, spot - 512)
    reach = class_count // 2 - 1
    label = jnp.clip(128 - spot, -reach, reach) + reach
    kind = lax.broadcasted_iota(jnp.int32, (512, class_count), 1)
    return (label == kind).astype(f32).astype(b16)


def forward_kernel(
    packed,
    tokens,
    cotangent,
    first_note,
    pair_note,
    ada_shard,
    tables,
    rows,
    output,
    held_out,
    h_one_out,
    qkv_out,
    probs_out,
    attended_out,
    proj_out,
    middle_out,
    h_two_out,
    gate_out,
    up_out,
    act_out,
    ada_out,
    d_gate_two_out,
    pre_out,
    note_out,
    pair_out,
    held,
    note_in,
    pair_in,
    part_rows,
    part_in,
    normed,
    h_one,
    qkv,
    bias,
    edges,
    probs,
    attended,
    proj,
    middle,
    h_two,
    gate,
    up,
    act,
    total,
    out_low,
    ring_send,
    ring_recv,
    side_send,
    side_recv,
    core_send,
    core_recv,
    note_send,
    note_recv,
    pair_send,
    pair_recv,
    part_send,
    part_recv,
    local_sem,
    probs_sem,
    out_sem,
):
    at = Place()
    gather = Gather(
        at, packed, held, (ring_send, ring_recv, side_send, side_recv, core_send, core_recv)
    )
    greet_all(at)

    def lead(index):
        for tau in range(sum(ahead_plan[:index]), sum(ahead_plan[: index + 1])):
            gather.tick(1 + tau)

    def note_copy(step, mine):
        other = lax.rem(at.me + step, 32)
        slot = at.me if mine else other
        return remote(
            first_note.at[lax.rem(other, 16)],
            note_in.at[slot],
            note_send.at[step],
            note_recv.at[slot],
            (lax.div(other, 16), lax.rem(other, 16)),
        )

    def pair_copy(step, mine):
        other = lax.rem(at.f + step, 16)
        slot = at.f if mine else other
        return remote(
            pair_note, pair_in.at[slot], pair_send.at[step], pair_recv.at[slot], (at.x, other)
        )

    def part_copy(step, mine):
        other = lax.rem(at.f + step, 16)
        slot = at.f if mine else other
        return remote(
            part_rows.at[other],
            part_in.at[slot],
            part_send.at[step],
            part_recv.at[slot],
            (at.x, other),
        )

    pl.loop(1, 32)(lambda step: note_copy(step, True).start())
    pl.loop(1, 16)(lambda step: pair_copy(step, True).start())
    for job in range(ahead + 1):
        gather.start(job)
    local = []
    for chunk in range(chunk_count):
        column = pl.ds(aligned(chunk * chunk_cols + at.x * side_cols), ring_cols)
        copy = pltpu.make_async_copy(
            packed.at[:, column], held.at[at.cy, at.c, :, column], local_sem.at[chunk]
        )
        copy.start()
        local.append(copy)
    note_in[at.me] = first_note[at.f]
    pair_in[at.f] = pair_note[...]
    values = tokens[...].astype(f32)
    centred = values - jnp.mean(values, axis=-1, keepdims=True)
    spread = jnp.mean(centred * centred, axis=-1, keepdims=True)
    normed[...] = centred * lax.rsqrt(spread + epsilon)
    for copy in local:
        copy.wait()
    lead(0)

    @pl.loop(1, 32)
    def _(step):
        note_copy(step, False).wait_recv()

    for window in range(32):
        note_out[window : window + 1, :] = note_in[window]
    notes = note_out[...]
    kind = lax.broadcasted_iota(jnp.int32, (32, tables.shape[1]), 1).astype(f32)
    hit = (kind == notes[:, 48:49]) | (kind == notes[:, 49:50]) | (kind == notes[:, 50:51])
    pre = notes[:, 0:48] + dot_nt(hit.astype(f32).astype(b16), tables[...])
    pre_out[...] = jnp.zeros_like(pre_out)
    pre_out[:, 0:48] = pre
    group = pre_out[pl.ds(pl.multiple_of(at.x * 16, 16), 16), :][:, 0:48]
    cond = (group * (1.0 / (1.0 + jnp.exp(-group)))).astype(b16)
    partial_rows = dot_nn(cond, ada_shard[...])
    for row in range(16):
        part_rows[row] = partial_rows[row : row + 1, :]
    lead(1)

    @pl.loop(1, 16)
    def _(step):
        pair_copy(step, False).wait_recv()

    gathered = pair_in[...].reshape(256, 384)
    features = gathered[:, 0:128].astype(f32)
    features = features - jnp.mean(features, axis=0, keepdims=True)
    features = features * lax.rsqrt(jnp.mean(features * features, axis=0, keepdims=True) + epsilon)
    table = dot_tn(gathered[:, 128:256], features.astype(b16))[0:16, :].astype(b16)
    table_wide = table.astype(f32)
    edges[0] = jnp.broadcast_to(table_wide[:, 126:127], (16, 128))
    edges[1] = jnp.broadcast_to(table_wide[:, 0:1], (16, 128))
    edges[2] = jnp.broadcast_to(table_wide[:, 127:128], (16, 128))
    spots = dot_nt(table, class_map(128))
    for head in range(12):
        line = jnp.broadcast_to(spots[head : head + 1, :], (128, 512))
        bias[head] = pltpu.roll(line, 0, 1, stride=1, stride_axis=0)[:, 0:384]
    pl.loop(1, 16)(lambda step: part_copy(step, True).start())
    lead(2)

    breaks = jnp.sum(pair_in[:, :, 256:384].astype(f32), axis=0)
    break_row = jnp.concatenate([breaks[row : row + 1, :] for row in range(6)], axis=1)
    mark_row = rows[1:2, :].astype(b16)
    lead(3)

    @pl.loop(1, 16)
    def _(step):
        part_copy(step, False).wait_recv()

    part_in[at.f] = part_rows[at.f]
    adaptive = part_in[0]
    for row in range(1, 16):
        adaptive = adaptive + part_in[row]
    ada_out[...] = adaptive
    shift_one = adaptive[:, 0:768]
    scale_one = adaptive[:, 768:1536]
    gate_one = adaptive[:, 1536:2304]
    shift_two = adaptive[:, 2304:3072]
    scale_two = adaptive[:, 3072:3840]
    gate_two = adaptive[:, 3840:4608]
    lead(4)
    first = normed[...] * (1.0 + scale_one) + shift_one
    h_one[...] = (first + dot_tn(mark_row, break_row.astype(b16))).astype(b16)
    outgoing = []

    def emit(src, dst):
        copy = pltpu.make_async_copy(src, dst, out_sem.at[len(outgoing)])
        copy.start()
        outgoing.append(copy)

    emit(h_one, h_one_out)
    emit(pair_in, pair_out)
    for tau in range(1 + sum(ahead_plan), 15):
        gather.tick(tau)

    def weights(column, width):
        return held[:, :, :, column : column + width].reshape(768, width)

    def settle(chunk):
        gather.arrive(chunk)
        column = pl.ds(chunk * chunk_cols, chunk_cols)
        emit(held.at[:, :, :, column], held_out.at[:, :, :, column])

    settle(0)
    for piece in range(3):
        span = slice(piece * 768, piece * 768 + 768)
        qkv[:, span] = dot_nn(h_one[...], weights(piece * 768, 768)).astype(b16)
        if piece < 2:
            gather.tick(15 + piece)
    emit(qkv, qkv_out)
    chain_row = rows[0:1, :]
    pad_row = rows[2:3, :]
    first_size = 512.0 - jnp.sum(chain_row, axis=1, keepdims=True)
    low_lane = lax.broadcasted_iota(jnp.int32, (1, 128), 1) < 64
    line_number = lax.broadcasted_iota(jnp.int32, (128, 128), 0).astype(f32)

    def probs_copy(pair):
        slot = modulo(pair, 2)
        return pltpu.make_async_copy(
            probs.at[slot], probs_out.at[pl.ds(pair * 2, 2)], probs_sem.at[slot]
        )

    @pl.loop(0, 6)
    def _(pair):
        lane = pl.multiple_of(pair * 128, 128)
        slot = lax.rem(pair, 2)
        on(pair >= 2, lambda: probs_copy(pair - 2).wait())
        queries = qkv[:, pl.ds(lane, 128)] * jnp.asarray(0.125, b16)
        keys = qkv[:, pl.ds(768 + lane, 128)]
        content = qkv[:, pl.ds(1536 + lane, 128)]
        mixed = []
        for half in range(2):
            head = pair * 2 + half
            own = low_lane if half == 0 else jnp.logical_not(low_lane)
            raw = dot_nt(jnp.where(own, queries, jnp.zeros_like(queries)), keys)
            far_low = edges[0, pl.ds(head, 1), :]
            far_high = edges[1, pl.ds(head, 1), :]
            apart = edges[2, pl.ds(head, 1), :]
            for block in range(4):
                chain_here = (line_number + 128.0 * block >= first_size).astype(f32)
                tiles = []
                for other in range(4):
                    offset = block - other
                    if offset > 1:
                        near = far_low
                    elif offset < -1:
                        near = far_high
                    else:
                        near = bias[head, :, (1 - offset) * 128 : (2 - offset) * 128]
                    there = chain_row[:, other * 128 : other * 128 + 128]
                    near = jnp.where(chain_here == there, near, apart)
                    tiles.append(
                        raw[block * 128 : block * 128 + 128, other * 128 : other * 128 + 128]
                        + near
                        + pad_row[:, other * 128 : other * 128 + 128]
                    )
                scores = jnp.concatenate(tiles, axis=1)
                scores = jnp.exp(scores - jnp.max(scores, axis=1, keepdims=True))
                scores = scores * (1.0 / jnp.sum(scores, axis=1, keepdims=True))
                probs[slot, half, block * 128 : block * 128 + 128, :] = scores.astype(b16)
            mixed.append(dot_nn(probs[slot, half], content))
        attended[:, pl.ds(lane, 128)] = jnp.where(low_lane, mixed[0], mixed[1]).astype(b16)
        probs_copy(pair).start()
        spot = 17 + pair + lax.div(pair, 2)
        gather.tick(spot)
        on(lax.rem(pair, 2) == 1, lambda: gather.tick(spot + 1))

    emit(attended, attended_out)
    projected = dot_nn(attended[...], weights(2304, 768))
    proj[...] = projected.astype(b16)
    middle[...] = tokens[...].astype(f32) + gate_one * projected
    emit(proj, proj_out)
    emit(middle, middle_out)
    gather.tick(26)
    values = middle[...]
    centred = values - jnp.mean(values, axis=-1, keepdims=True)
    spread = jnp.mean(centred * centred, axis=-1, keepdims=True)
    second = centred * lax.rsqrt(spread + epsilon) * (1.0 + scale_two) + shift_two
    h_two[...] = second.astype(b16)
    emit(h_two, h_two_out)
    gather.tick(27)

    settle(1)

    def moving(column):
        return held[:, :, :, pl.ds(pl.multiple_of(column, 128), 768)].reshape(768, 768)

    @pl.loop(0, 4)
    def _(piece):
        span = pl.ds(pl.multiple_of(piece * 768, 128), 768)
        gate[:, span] = dot_nn(h_two[...], moving(3072 + piece * 768)).astype(b16)
        on(lax.rem(piece, 2) == 1, lambda: gather.tick(28 + lax.div(piece, 2)))

    emit(gate, gate_out)
    settle(2)

    @pl.loop(0, 4)
    def _(piece):
        span = pl.ds(pl.multiple_of(piece * 768, 128), 768)
        raised = dot_nn(h_two[...], moving(6144 + piece * 768))
        gated = gate[:, span].astype(f32)
        up[:, span] = raised.astype(b16)
        act[:, span] = (gated * (1.0 / (1.0 + jnp.exp(-gated))) * raised).astype(b16)
        on(piece < 3, lambda: gather.tick(30 + piece))

    emit(up, up_out)
    emit(act, act_out)
    settle(3)
    total[...] = dot_nt(act[...], weights(9216, 3072))
    fed = total[...]
    d_gate_two_out[...] = jnp.sum(cotangent[...].astype(f32) * fed, axis=0, keepdims=True)
    out_low[...] = (middle[...] + gate_two * fed).astype(b16)
    emit(out_low, output)

    probs_copy(4).wait()
    probs_copy(5).wait()
    gather.finish()
    for copy in outgoing:
        copy.wait()

    @pl.loop(1, 32)
    def _(step):
        note_copy(step, True).wait_send()

    @pl.loop(1, 16)
    def _(step):
        pair_copy(step, True).wait_send()
        part_copy(step, True).wait_send()


def run_forward(packed, tokens, cotangent, first_note, pair_note, ada_shard, tables, rows):
    anywhere = pl.BlockSpec(memory_space=pl.ANY)
    near = pl.BlockSpec(memory_space=pltpu.VMEM)
    shape = jax.ShapeDtypeStruct
    dma = pltpu.SemaphoreType.DMA
    vmem = pltpu.VMEM
    width = 768
    outs = [
        (shape((512, width), b16), anywhere),
        (shape((8, 2, 48, 12288), b16), anywhere),
        (shape((512, width), b16), anywhere),
        (shape((512, 3 * width), b16), anywhere),
        (shape((12, 512, 512), b16), anywhere),
        (shape((512, width), b16), anywhere),
        (shape((512, width), b16), anywhere),
        (shape((512, width), f32), anywhere),
        (shape((512, width), b16), anywhere),
        (shape((512, 3072), b16), anywhere),
        (shape((512, 3072), b16), anywhere),
        (shape((512, 3072), b16), anywhere),
        (shape((1, 4608), f32), near),
        (shape((1, width), f32), near),
        (shape((32, 128), f32), near),
        (shape((32, 128), f32), near),
        (shape((16, 16, 384), b16), anywhere),
    ]
    scratch = [
        vmem((8, 2, 48, 12288), b16),
        vmem((32, 1, 128), f32),
        vmem((16, 16, 384), b16),
        vmem((16, 1, 4608), f32),
        vmem((16, 1, 4608), f32),
        vmem((512, width), f32),
        vmem((512, width), b16),
        vmem((512, 3 * width), b16),
        vmem((12, 128, 384), f32),
        vmem((3, 16, 128), f32),
        vmem((2, 2, 512, 512), b16),
        vmem((512, width), b16),
        vmem((512, width), b16),
        vmem((512, width), f32),
        vmem((512, width), b16),
        vmem((512, 3072), b16),
        vmem((512, 3072), b16),
        vmem((512, 3072), b16),
        vmem((512, width), f32),
        vmem((512, width), b16),
        dma((job_count, 4, 2)),
        dma((job_count, 4, 2)),
        dma((8,)),
        dma((8,)),
        dma((8,)),
        dma((8,)),
        dma((32,)),
        dma((32,)),
        dma((16,)),
        dma((16,)),
        dma((16,)),
        dma((16,)),
        dma((4,)),
        dma((2,)),
        dma((24,)),
    ]
    return pl.pallas_call(
        forward_kernel,
        name="forward",
        out_shape=[one for one, _ in outs],
        in_specs=[anywhere] + [near] * 7,
        out_specs=[spec for _, spec in outs],
        scratch_shapes=scratch,
        compiler_params=pltpu.CompilerParams(
            collective_id=0, has_side_effects=True, vmem_limit_bytes=66_000_000
        ),
    )(packed, tokens, cotangent, first_note, pair_note, ada_shard, tables, rows)


side_jobs = 2
messages_in_job = 7


class Scatter:
    def __init__(self, at, grads, ring_in, core_in, side_in, last_in, summed, sems):
        self.at = at
        self.grads = grads
        self.ring_in = ring_in
        self.core_in = core_in
        self.side_in = side_in
        self.last_in = last_in
        self.summed = summed
        self.now = 0
        self.begun = []
        (
            self.ring_send,
            self.ring_recv,
            self.core_send,
            self.core_recv,
            self.side_send,
            self.side_recv,
            self.last_send,
            self.last_recv,
            self.credit,
        ) = sems

    def column(self, job, owner):
        inner = modulo(job, jobs_in_chunk)
        outer = quot(inner, 4)
        return aligned(inner * job_cols + side_cols + outer * (owner * ring_cols - ring_cols))

    def block(self, job, position):
        at = self.at
        buffer = modulo(quot(job, jobs_in_chunk), grad_buffers)
        span = pl.ds(self.column(job, at.x), job_cols)
        return self.grads.at[buffer, at.chip(position), at.c, :, span]

    def slot(self, job, step, way):
        return job * messages_in_job + (0 if step == 0 else 2 * step - 1 + way)

    def ring(self, job, step, way):
        at = self.at
        sign = 1 - 2 * way
        slot = self.slot(job, step, way)
        return remote(
            self.block(job, at.p + (4 - step) * sign),
            self.ring_in.at[slot],
            self.ring_send.at[slot],
            self.ring_recv.at[slot],
            at.ring_id(at.p + sign),
        )

    def absorb(self, job, step, way):
        self.ring(job, step, way).wait_recv()
        sign = 1 - 2 * way
        own = self.block(job, self.at.p + (3 - step) * sign)
        came = self.ring_in[self.slot(job, step, way)]
        own[...] = (own[...].astype(f32) + came.astype(f32)).astype(b16)

    def core(self, turn, piece):
        at = self.at
        span = pl.ds(aligned(piece * side_cols), side_cols)
        return remote(
            self.grads.at[turn % grad_buffers, :, 1 - at.c, :, span],
            self.core_in.at[turn % 2, piece],
            self.core_send.at[turn, piece],
            self.core_recv.at[turn, piece],
            at.core_id(),
        )

    def core_start(self, turn, piece):
        if turn >= 2:
            pl.semaphore_wait(self.credit.at[turn % 2, piece], 1)
        self.core(turn, piece).start()

    def core_add(self, turn, piece):
        at = self.at
        self.core(turn, piece).wait_recv()
        span = pl.ds(piece * side_cols, side_cols)

        @pl.loop(0, chip_count)
        def _(chip):
            own = self.grads.at[turn % grad_buffers, chip, at.c, :, span]
            came = self.core_in[turn % 2, piece, chip]
            own[...] = (own[...].astype(f32) + came.astype(f32)).astype(b16)

        if turn < 2:
            pl.semaphore_signal(
                self.credit.at[turn % 2, piece],
                inc=1,
                device_id=at.core_id(),
                device_id_type=mesh_ids,
            )

    def side(self, turn, half):
        at = self.at
        span = pl.ds(aligned((1 - at.x) * ring_cols + half * job_cols), job_cols)
        slot = turn * side_jobs + half
        return remote(
            self.grads.at[modulo(turn, grad_buffers), :, at.c, :, span],
            self.side_in.at[slot],
            self.side_send.at[slot],
            self.side_recv.at[slot],
            at.plane_id(),
        )

    def side_add(self, turn, half):
        at = self.at
        self.side(turn, half).wait_recv()
        span = pl.ds(aligned(at.x * ring_cols + half * job_cols), job_cols)

        @pl.loop(0, chip_count)
        def _(chip):
            own = self.grads.at[modulo(turn, grad_buffers), chip, at.c, :, span]
            came = self.side_in[turn * side_jobs + half, chip]
            own[...] = (own[...].astype(f32) + came.astype(f32)).astype(b16)

    def last(self, job):
        return remote(
            self.block(job, self.at.p),
            self.last_in.at[job],
            self.last_send.at[job],
            self.last_recv.at[job],
            self.at.plane_id(),
        )

    def store(self, job):
        at = self.at
        self.last(job).wait_recv()
        turn = quot(job, jobs_in_chunk)
        inner = modulo(job, jobs_in_chunk)
        if isinstance(job, int):
            chunk = (3, 1, 2, 0)[turn]
        else:
            chunk = turn + 3 * (1 - jnp.minimum(turn, 1)) - 3 * lax.div(turn, 3)
        base = chunk * chunk_cols
        mine = self.block(job, at.p)[...].astype(f32)
        other = self.last_in[job].astype(f32)

        def whole():
            span = pl.ds(aligned(base + self.column(job, at.x)), job_cols)
            self.summed[:, span] = mine + other

        def halves():
            span = pl.ds(aligned(base + self.column(job, at.x)), job_cols)
            self.summed[:, span] = mine
            span = pl.ds(aligned(base + self.column(job, 1 - at.x)), job_cols)
            self.summed[:, span] = other

        on(inner < 4, whole)
        on(inner >= 4, halves)

    def begin(self, turn, beside, wait=0):
        first = self.now + wait
        assert not self.begun or first >= self.begun[-1][0] + self.begun[-1][2]
        base = turn * jobs_in_chunk
        self.begun.append((first, base + 4, 2) if beside else (first, base, 4))

    def step(self, count=1):
        for _ in range(count):
            self.tick(self.now)
            self.now += 1

    def drain(self):
        last = self.begun[-1][0] + 2 + 4 * scatter_stride + 2
        pl.loop(self.now, last)(self.tick)
        self.now = last

    def tick(self, tau):
        def each(age, body):
            spot = tau - age
            if isinstance(spot, int):
                for first, base, count in self.begun:
                    if 0 <= spot - first < count:
                        body(base + spot - first)
                return
            job = jnp.int32(-1)
            for first, base, count in self.begun:
                inside = jnp.logical_and(spot >= first, spot < first + count)
                job = jnp.where(inside, spot - first + base, job)
            pl.when(job >= 0)(lambda: body(job))

        def two(step, body):
            def run(job):
                body(job, step, 0)
                body(job, step, 1)

            return run

        def start(job, step, way):
            self.ring(job, step, way).start()

        gap = scatter_stride
        each(4 * gap, two(3, self.absorb))
        each(3 * gap, two(2, self.absorb))
        each(2 * gap, two(1, self.absorb))
        each(gap, lambda job: self.absorb(job, 0, modulo(job, 2)))

        def beside(job):
            inner = modulo(job, jobs_in_chunk)
            turn = quot(job, jobs_in_chunk)
            on(inner == 4, lambda: self.side_add(turn, 0))
            on(inner == 5, lambda: self.side_add(turn, 1))

        each(0, beside)
        each(3 * gap, two(3, start))
        each(2 * gap, two(2, start))
        each(gap, two(1, start))
        each(0, lambda job: start(job, 0, modulo(job, 2)))
        each(4 * gap, lambda job: self.last(job).start())
        each(4 * gap + 2, self.store)

    def sent(self, turns):
        @pl.loop(turns[0] * jobs_in_chunk, turns[-1] * jobs_in_chunk + jobs_in_chunk)
        def _(job):
            self.ring(job, 0, lax.rem(job, 2)).wait_send()
            for step in range(1, 4):
                self.ring(job, step, 0).wait_send()
                self.ring(job, step, 1).wait_send()
            self.last(job).wait_send()

        for turn in turns:
            for piece in range(4):
                self.core(turn, piece).wait_send()
            for half in range(2):
                self.side(turn, half).wait_send()


def halves_of(values):
    high = values.astype(b16)
    return high, (values - high.astype(f32)).astype(b16)


def backward_kernel(
    held,
    probs_all,
    h_one_all,
    qkv_all,
    attended_all,
    proj_all,
    middle_all,
    h_two_all,
    gate_all,
    up_all,
    act_all,
    tokens_all,
    cotangent_all,
    adaptive,
    d_gate_two,
    pre_all,
    notes,
    pair_all,
    ada_shard,
    rows,
    d_tokens_out,
    summed,
    grad_ada,
    grad_tables,
    grad_pair,
    grad_proj,
    grad_break,
    grads,
    ring_in,
    core_in,
    side_in,
    last_in,
    piece_in,
    probs,
    d_scores,
    cot,
    act,
    gate,
    up,
    hidden,
    mid,
    d_mid,
    d_hid,
    proj,
    low,
    sums,
    lines,
    far,
    note_wide,
    note_low,
    vector_in,
    vector_wide,
    d_ada_all,
    pair_work,
    ring_send,
    ring_recv,
    core_send,
    core_recv,
    side_send,
    side_recv,
    last_send,
    last_recv,
    credit,
    load_sem,
    piece_sem,
    probs_sem,
    vector_send,
    vector_recv,
    share_send,
    share_recv,
):
    at = Place()
    scatter = Scatter(
        at,
        grads,
        ring_in,
        core_in,
        side_in,
        last_in,
        summed,
        (
            ring_send,
            ring_recv,
            core_send,
            core_recv,
            side_send,
            side_recv,
            last_send,
            last_recv,
            credit,
        ),
    )
    loads = []

    def load(src, dst):
        copy = pltpu.make_async_copy(src, dst, load_sem.at[len(loads)])
        copy.start()
        loads.append(copy)
        return copy

    cot_load = load(cotangent_all, cot)
    act_load = load(act_all, act)
    piece_order = [9216 + 768 * n for n in range(4)]
    for n in range(4):
        piece_order += [3072 + 768 * n, 6144 + 768 * n]
    piece_order += [2304, 0, 768, 1536]

    def piece_copy(index):
        if isinstance(index, int):
            column = pl.ds(piece_order[index], side_cols)
        else:
            inner = index - 4
            start = 3072 + 768 * lax.div(inner, 2) + 3072 * lax.rem(inner, 2)
            start = jnp.where(index < 4, 9216 + 768 * index, start)
            start = jnp.where(index == 12, 2304, start)
            start = jnp.where(index > 12, (index - 13) * 768, start)
            column = pl.ds(pl.multiple_of(start, 128), side_cols)
        index = modulo(index, 4)
        return pltpu.make_async_copy(
            held.at[:, :, :, column], piece_in.at[index], piece_sem.at[index]
        )

    def piece(index):
        piece_copy(index).wait()
        return piece_in[modulo(index, 4)].reshape(768, 768)

    def piece_used(index):
        on(index + 4 < len(piece_order), lambda: piece_copy(index + 4).start())

    for index in range(4):
        piece_copy(index).start()
    gate_load = load(gate_all, gate)
    up_load = load(up_all, up)
    hidden_load = load(h_two_all, hidden)
    mid_load = load(middle_all, mid)
    proj_load = load(proj_all, proj)

    def probs_copy(pair):
        slot = modulo(pair, 2)
        return pltpu.make_async_copy(
            probs_all.at[pl.ds(pair * 2, 2)], probs.at[slot], probs_sem.at[slot]
        )

    probs_copy(0).start()
    probs_copy(1).start()
    greet_all(at)
    scale_one = adaptive[:, 768:1536]
    gate_one = adaptive[:, 1536:2304]
    scale_two = adaptive[:, 3072:3840]
    gate_two = adaptive[:, 3840:4608]
    sums[...] = jnp.zeros_like(sums)

    def columns(part):
        return pl.ds(aligned(part * 768), 768)

    def put(turn, part, left, right):
        span = columns(part)
        grads[turn % grad_buffers, :, :, :, span] = (
            dot_tn(left, right).astype(b16).reshape(8, 2, 48, 768)
        )
        scatter.core_start(turn, part)

    def merge(turn):
        scatter.core_add(turn, 0)
        scatter.core_add(turn, 3)
        scatter.side(turn, 0).start()
        scatter.side(turn, 1).start()
        scatter.core_add(turn, 1)
        scatter.core_add(turn, 2)
        scatter.begin(turn, False)

    cot_load.wait()
    low[...] = (gate_two * cot[...].astype(f32)).astype(b16)
    act_load.wait()

    @pl.loop(0, 4)
    def _(index):
        part = lax.rem(3 * index, 4)
        put(0, part, low[...], act[:, columns(part)])

    qkv_load = load(qkv_all, act.at[:, 0:2304])
    attended_load = load(attended_all, act.at[:, 2304:3072])
    gate_load.wait()
    up_load.wait()

    def first_part():
        merge(0)

    @pl.loop(0, 4)
    def _(part):
        d_hid[...] = dot_nn(low[...], piece(part))
        piece_used(part)
        span = columns(part)

        @pl.loop(0, 8)
        def _(block):
            line = pl.ds(pl.multiple_of(block * 64, 64), 64)
            d_act = d_hid[line, :]
            gated = gate[line, span].astype(f32)
            raised = up[line, span].astype(f32)
            sigma = 1.0 / (1.0 + jnp.exp(-gated))
            scaled = d_act * sigma
            gate[line, span] = (scaled * raised * (1.0 + gated * (1.0 - sigma))).astype(b16)
            up[line, span] = (scaled * gated).astype(b16)

        on(part == 0, first_part)
        scatter.tick(scatter.now + part)

    scatter.now += 4
    hidden_load.wait()

    @pl.loop(0, 4)
    def _(index):
        part = lax.rem(3 * index, 4)
        put(1, part, hidden[...], gate[:, columns(part)])
        on(index == 1, lambda: scatter.tick(scatter.now))

    scatter.now += 1
    scatter.step(plan[1])

    def second_part():
        merge(1)
        scatter.begin(0, True, 4)
        scatter.tick(scatter.now)

    @pl.loop(0, 4)
    def _(index):
        part = lax.rem(3 * index, 4)
        put(2, part, hidden[...], up[:, columns(part)])
        on(index == 1, second_part)

    scatter.now += 1
    scatter.step(plan[2])
    h_one_load = load(h_one_all, hidden)
    d_hid[...] = jnp.zeros_like(d_hid)

    @pl.loop(0, 4)
    def _(part):
        span = columns(part)
        d_hid[...] += dot_nt(gate[:, span], piece(4 + 2 * part))
        piece_used(4 + 2 * part)
        d_hid[...] += dot_nt(up[:, span], piece(5 + 2 * part))
        piece_used(5 + 2 * part)
        scatter.tick(scatter.now + part)

    scatter.now += 4
    merge(2)
    scatter.begin(1, True, 4)
    scatter.begin(2, True, 12)
    mid_load.wait()
    proj_load.wait()

    @pl.loop(0, 8)
    def _(block):
        line = pl.ds(pl.multiple_of(block * 64, 64), 64)
        values = mid[line, :]
        centred = values - jnp.mean(values, axis=-1, keepdims=True)
        inverse = lax.rsqrt(jnp.mean(centred * centred, axis=-1, keepdims=True) + epsilon)
        centred = centred * inverse
        grad = d_hid[line, :]
        sums[0:1, :] += jnp.sum(grad, axis=0, keepdims=True)
        sums[1:2, :] += jnp.sum(grad * centred, axis=0, keepdims=True)
        grad = grad * (1.0 + scale_two)
        grad = grad - jnp.mean(grad, axis=-1, keepdims=True) - centred * jnp.mean(
            grad * centred, axis=-1, keepdims=True
        )
        grad = cot[line, :].astype(f32) + inverse * grad
        d_mid[line, :] = grad
        sums[2:3, :] += jnp.sum(grad * proj[line, :].astype(f32), axis=0, keepdims=True)
        low[line, :] = (gate_one * grad).astype(b16)

    tokens_load = load(tokens_all, proj)
    scatter.step(plan[4])
    cot[...] = dot_nt(low[...], piece(12)).astype(b16)
    piece_used(12)
    qkv_load.wait()
    attended_load.wait()
    scatter.step(plan[4])
    start_tick = scatter.now

    chain_row = rows[0:1, :]
    first_size = 512.0 - jnp.sum(chain_row, axis=1, keepdims=True)
    low_lane = lax.broadcasted_iota(jnp.int32, (1, 128), 1) < 64
    line_number = lax.broadcasted_iota(jnp.int32, (128, 128), 0).astype(f32)
    lines[...] = jnp.zeros_like(lines)
    far[...] = jnp.zeros_like(far)

    @pl.loop(0, 6)
    def _(pair):
        lane = pl.multiple_of(pair * 128, 128)
        slot = lax.rem(pair, 2)
        probs_copy(pair).wait()
        queries = act[:, pl.ds(lane, 128)] * jnp.asarray(0.125, b16)
        keys = act[:, pl.ds(768 + lane, 128)]
        content = act[:, pl.ds(1536 + lane, 128)]
        d_out = cot[:, pl.ds(lane, 128)]
        d_queries, d_keys, d_content = [], [], []
        for half in range(2):
            head = pair * 2 + half
            own = low_lane if half == 0 else jnp.logical_not(low_lane)
            d_own = jnp.where(own, d_out, jnp.zeros_like(d_out))
            d_probs = dot_nt(d_own, content)
            band = [None, None, None]
            low_sum = jnp.zeros((128, 128), f32)
            high_sum = jnp.zeros((128, 128), f32)
            apart = jnp.zeros((128, 128), f32)
            for block in range(4):
                line = slice(block * 128, block * 128 + 128)
                here = probs[slot, half, line, :].astype(f32)
                weighted = here * d_probs[line, :]
                weighted = weighted - here * jnp.sum(weighted, axis=1, keepdims=True)
                d_scores[line, :] = weighted.astype(b16)
                chain_here = (line_number + 128.0 * block >= first_size).astype(f32)
                for other in range(4):
                    tile = weighted[:, other * 128 : other * 128 + 128]
                    there = chain_row[:, other * 128 : other * 128 + 128]
                    same = jnp.where(chain_here == there, tile, jnp.zeros_like(tile))
                    apart = apart + (tile - same)
                    offset = block - other
                    if offset > 1:
                        low_sum = low_sum + same
                    elif offset < -1:
                        high_sum = high_sum + same
                    elif band[1 - offset] is None:
                        band[1 - offset] = same
                    else:
                        band[1 - offset] = band[1 - offset] + same
            far[0, pl.ds(head, 1), :] = jnp.sum(low_sum, axis=0, keepdims=True)
            far[1, pl.ds(head, 1), :] = jnp.sum(high_sum, axis=0, keepdims=True)
            far[2, pl.ds(head, 1), :] = jnp.sum(apart, axis=0, keepdims=True)
            folded = jnp.concatenate(band + [jnp.zeros((128, 128), f32)], axis=1)
            size = 64
            while size >= 1:
                folded = folded[0:size, :] + pltpu.roll(
                    folded[size : 2 * size, :], 512 - size, 1
                )
                size = size // 2
            lines[pl.ds(head, 1), :] = folded
            d_here = d_scores[...]
            d_queries.append(dot_nn(d_here, keys))
            masked = jnp.where(own, queries, jnp.zeros_like(queries))
            d_keys.append(dot_tn(d_here, masked))
            d_content.append(dot_tn(probs[slot, half], d_own))
            if half == 0:
                for extra in range(plan[5]):
                    scatter.tick(start_tick + (plan[5] + plan[6]) * pair + extra)
        gate[:, pl.ds(lane, 128)] = (
            jnp.where(low_lane, d_queries[0], d_queries[1]) * 0.125
        ).astype(b16)
        gate[:, pl.ds(768 + lane, 128)] = (d_keys[0] + d_keys[1]).astype(b16)
        gate[:, pl.ds(1536 + lane, 128)] = (d_content[0] + d_content[1]).astype(b16)
        on(pair < 4, lambda: probs_copy(pair + 2).start())
        for extra in range(plan[6]):
            scatter.tick(start_tick + (plan[5] + plan[6]) * pair + plan[5] + extra)

    scatter.now += 6 * (plan[5] + plan[6])
    if grad_buffers == 3:
        done = scatter.begun[2][0] + 2 + 4 * scatter_stride + 2
        assert scatter.now >= done and scatter.begun[2][1] == 4
        scatter.sent([0])
    put(3, 3, act[:, 2304:3072], low[...])
    h_one_load.wait()
    put(3, 0, hidden[...], gate[:, 0:768])
    scatter.step(plan[7])
    put(3, 1, hidden[...], gate[:, 768:1536])
    put(3, 2, hidden[...], gate[:, 1536:2304])
    for part in range(3):
        product = dot_nt(gate[:, part * 768 : part * 768 + 768], piece(13 + part))
        if part == 0:
            d_hid[...] = product
        else:
            d_hid[...] += product
        if part == 0:
            merge(3)
            scatter.begin(3, True, plan[10])
        scatter.step(plan[8])
    tokens_load.wait()

    @pl.loop(0, 8)
    def _(block):
        line = pl.ds(pl.multiple_of(block * 64, 64), 64)
        values = proj[line, :].astype(f32)
        centred = values - jnp.mean(values, axis=-1, keepdims=True)
        inverse = lax.rsqrt(jnp.mean(centred * centred, axis=-1, keepdims=True) + epsilon)
        centred = centred * inverse
        grad = d_hid[line, :]
        sums[3:4, :] += jnp.sum(grad, axis=0, keepdims=True)
        sums[4:5, :] += jnp.sum(grad * centred, axis=0, keepdims=True)
        cot[line, :] = grad.astype(b16)
        grad = grad * (1.0 + scale_one)
        grad = grad - jnp.mean(grad, axis=-1, keepdims=True) - centred * jnp.mean(
            grad * centred, axis=-1, keepdims=True
        )
        low[line, :] = (d_mid[line, :] + inverse * grad).astype(b16)

    tokens_store = load(low, d_tokens_out)
    break_sum = dot_nn(jnp.broadcast_to(rows[1:2, :], (8, 512)).astype(b16), cot[...])
    scatter.step(plan[9])

    scale = class_map(128)
    line_high, line_low = halves_of(lines[...])
    d_table = dot_nn(line_high, scale) + dot_nn(line_low, scale)
    kind = lax.broadcasted_iota(jnp.int32, (16, 128), 1)
    for index, label in ((0, 126), (1, 0), (2, 127)):
        total = jnp.sum(far[index], axis=1, keepdims=True)
        d_table = d_table + jnp.where(kind == label, total, jnp.zeros_like(d_table))
    vectors = [sums[3:4, :], sums[4:5, :], sums[2:3, :], sums[0:1, :], sums[1:2, :]]
    vectors.append(d_gate_two[...])
    for index in range(6):
        for part in range(6):
            note_wide[index * 6 + part : index * 6 + part + 1, :] = vectors[index][
                :, part * 128 : part * 128 + 128
            ]
    note_wide[36:48, :] = d_table[0:12, :]
    for part in range(6):
        note_wide[48 + part : 49 + part, :] = break_sum[0:1, part * 128 : part * 128 + 128]
    note_wide[54:64, :] = jnp.zeros((10, 128), f32)
    note_low[...] = note_wide[...].astype(b16)
    vector_in[at.x, at.cy, at.c] = note_low[...]
    scatter.step(plan[9])

    def vector_copy(step, mine):
        other = lax.rem(at.cy + step, 8)
        slot = at.cy if mine else other
        return remote(
            note_low,
            vector_in.at[at.x, slot, at.c],
            vector_send.at[step],
            vector_recv.at[slot],
            (at.x, other * 2 + at.c),
        )

    def plane_copy(plane):
        block = vector_in.at[plane, :, at.c]
        return remote(block, block, share_send.at[0], share_recv.at[0], at.plane_id())

    def pair_copy(core):
        block = vector_in.at[:, :, core]
        return remote(block, block, share_send.at[1], share_recv.at[1], at.core_id())

    for step in range(1, 8):
        vector_copy(step, True).start()
    scatter.step(plan[9])
    for step in range(1, 8):
        vector_copy(step, False).wait_recv()
    plane_copy(at.x).start()
    scatter.step(plan[9])
    plane_copy(1 - at.x).wait_recv()
    pair_copy(at.c).start()
    scatter.step(plan[9])
    pair_copy(1 - at.c).wait_recv()
    total = jnp.zeros((64, 128), f32)
    for plane in range(2):
        vector_wide[...] = vector_in[plane].reshape(1024, 128).astype(f32)
        for part in range(36):
            d_ada_all[plane * 16 : plane * 16 + 16, part * 128 : part * 128 + 128] = vector_wide[
                pl.ds(part, 16, stride=64), :
            ].astype(b16)
        for window in range(16):
            total = total + vector_wide[window * 64 : window * 64 + 64, :]
    note_wide[...] = total
    pre = pre_all[...]
    sigma = 1.0 / (1.0 + jnp.exp(-pre))
    grad_ada[...] = dot_tn((pre * sigma).astype(b16)[:, 0:48], d_ada_all[...])
    d_pre = dot_nt(d_ada_all[...], ada_shard[...])
    pre, sigma = pre[:, 0:48], sigma[:, 0:48]
    d_pre = d_pre * sigma * (1.0 + pre * (1.0 - sigma))
    scatter.step(plan[9])
    labels = notes[...]
    kind = lax.broadcasted_iota(jnp.int32, (32, grad_tables.shape[1]), 1).astype(f32)
    hit = (kind == labels[:, 48:49]) | (kind == labels[:, 49:50]) | (kind == labels[:, 50:51])
    hit = hit.astype(f32).astype(b16)
    high, rest = halves_of(d_pre)
    grad_tables[...] = dot_tn(high, hit) + dot_tn(rest, hit)
    scatter.step(plan[9])
    grad_break[...] = note_wide[48:56, :]
    d_table = note_wide[36:52, :]
    keep = lax.broadcasted_iota(jnp.int32, (16, 128), 0) < 12
    d_table = jnp.where(keep, d_table, jnp.zeros_like(d_table))
    gathered = pair_all[...].reshape(256, 384)
    features = gathered[:, 0:128].astype(f32)
    features = features - jnp.mean(features, axis=0, keepdims=True)
    inverse = lax.rsqrt(jnp.mean(features * features, axis=0, keepdims=True) + epsilon)
    features = features * inverse
    high, rest = halves_of(d_table)
    pair_low = features.astype(b16)
    pair_work[:, 0:16] = dot_nt(pair_low, high) + dot_nt(pair_low, rest)
    mine = pl.ds(pl.multiple_of(at.f * 16, 16), 16)
    grad_proj[...] = pair_work[mine, :]
    weights = gathered[:, 128:144]
    grad = dot_nn(weights, high) + dot_nn(weights, rest)
    grad = inverse * (
        grad
        - jnp.mean(grad, axis=0, keepdims=True)
        - features * jnp.mean(grad * features, axis=0, keepdims=True)
    )
    pair_work[...] = grad
    grad_pair[...] = pair_work[mine, :]
    scatter.drain()
    scatter.sent([1, 2, 3] if grad_buffers == 3 else [0, 1, 2, 3])
    tokens_store.wait()
    for step in range(1, 8):
        vector_copy(step, True).wait_send()
    plane_copy(at.x).wait_send()
    pair_copy(at.c).wait_send()


def run_backward(saved, tokens, cotangent, ada_shard, rows, table_rows):
    (
        held,
        h_one,
        qkv,
        probs,
        attended,
        proj,
        middle,
        h_two,
        gate,
        up,
        act,
        adaptive,
        d_gate_two,
        pre,
        notes,
        pair_all,
    ) = saved
    anywhere = pl.BlockSpec(memory_space=pl.ANY)
    near = pl.BlockSpec(memory_space=pltpu.VMEM)
    shape = jax.ShapeDtypeStruct
    dma = pltpu.SemaphoreType.DMA
    vmem = pltpu.VMEM
    width = 768
    outs = [
        (shape((512, width), b16), anywhere),
        (shape((48, 12288), f32), near),
        (shape((48, 4608), f32), near),
        (shape((48, table_rows), f32), near),
        (shape((16, 128), f32), near),
        (shape((16, 128), f32), near),
        (shape((8, 128), f32), near),
    ]
    ring_slots = job_count * messages_in_job
    scratch = [
        vmem((grad_buffers, 8, 2, 48, chunk_cols), b16),
        vmem((ring_slots, 48, job_cols), b16),
        vmem((2, 4, 8, 48, side_cols), b16),
        vmem((8, 8, 48, job_cols), b16),
        vmem((job_count, 48, job_cols), b16),
        vmem((4, 8, 2, 48, side_cols), b16),
        vmem((2, 2, 512, 512), b16),
        vmem((512, 512), b16),
        vmem((512, width), b16),
        vmem((512, 3072), b16),
        vmem((512, 3072), b16),
        vmem((512, 3072), b16),
        vmem((512, width), b16),
        vmem((512, width), f32),
        vmem((512, width), f32),
        vmem((512, width), f32),
        vmem((512, width), b16),
        vmem((512, width), b16),
        vmem((8, width), f32),
        vmem((16, 512), f32),
        vmem((3, 16, 128), f32),
        vmem((64, 128), f32),
        vmem((64, 128), b16),
        vmem((2, 8, 2, 64, 128), b16),
        vmem((1024, 128), f32),
        vmem((32, 4608), b16),
        vmem((256, 128), f32),
        dma((ring_slots,)),
        dma((ring_slots,)),
        dma((4, 4)),
        dma((4, 4)),
        dma((8,)),
        dma((8,)),
        dma((job_count,)),
        dma((job_count,)),
        pltpu.SemaphoreType.REGULAR((2, 4)),
        dma((16,)),
        dma((4,)),
        dma((2,)),
        dma((8,)),
        dma((8,)),
        dma((2,)),
        dma((2,)),
    ]
    return pl.pallas_call(
        backward_kernel,
        name="backward",
        out_shape=[one for one, _ in outs],
        in_specs=[anywhere] * 13 + [near] * 7,
        out_specs=[spec for _, spec in outs],
        scratch_shapes=scratch,
        compiler_params=pltpu.CompilerParams(
            collective_id=1, has_side_effects=True, vmem_limit_bytes=67_043_328
        ),
    )(
        held,
        probs,
        h_one,
        qkv,
        attended,
        proj,
        middle,
        h_two,
        gate,
        up,
        act,
        tokens,
        cotangent,
        adaptive,
        d_gate_two,
        pre,
        notes,
        pair_all,
        ada_shard,
        rows,
    )


def pack_kernel(
    time_embed,
    cath_class,
    cath_arch,
    cath_topo,
    res_counts,
    chain_ids,
    break_mask,
    w_qkv,
    w_out,
    w_gate,
    w_up,
    w_down,
    table_class,
    table_arch,
    table_topo,
    break_vec,
    pair_table,
    pair_proj,
    packed,
    first_note,
    pair_note,
    tables,
    rows,
):
    packed[:, 0:2304] = w_qkv[...]
    packed[:, 2304:3072] = w_out[...]
    packed[:, 3072:6144] = w_gate[...]
    packed[:, 6144:9216] = w_up[...]
    packed[:, 9216:12288] = w_down[...]
    lane = lax.broadcasted_iota(jnp.int32, (1, 128), 1)
    marks = jnp.zeros((1, 128), f32)
    for index, labels in enumerate((cath_class, cath_arch, cath_topo)):
        label = (labels[0] + 128 * index).astype(f32)
        marks = jnp.where(lane == 48 + index, label, marks)
    embed = time_embed[...].astype(f32)
    for owner in range(16):
        first_note[owner] = marks
        first_note[owner, :, 0:48] = embed[:, owner * 48 : owner * 48 + 48]
    shard = lax.axis_index("fsdp") * 48
    unit = lax.broadcasted_iota(jnp.int32, (128, 128), 0)
    unit = (unit == lax.broadcasted_iota(jnp.int32, (128, 128), 1)).astype(f32).astype(b16)
    pair_note[:, 0:128] = pair_table[...]
    pair_note[:, 128:256] = jnp.zeros((16, 128), b16)
    pair_note[:, 128:140] = pair_proj[...]
    spot = lax.broadcasted_iota(jnp.int32, (48, 2048), 1) - shard
    spot = (spot == lax.broadcasted_iota(jnp.int32, (48, 2048), 0)).astype(f32).astype(b16)
    placed = dot_nn(jnp.broadcast_to(break_vec[...].astype(f32), (16, 48)).astype(b16), spot)
    line = lax.broadcasted_iota(jnp.int32, (16, 128), 0)
    breaks = jnp.zeros((16, 128), f32)
    for row in range(16):
        breaks = jnp.where(line == row, placed[:, row * 128 : row * 128 + 128], breaks)
    pair_note[:, 256:384] = breaks.astype(b16)
    for index, lookup in enumerate((table_class, table_arch)):
        block = dot_tn(lookup[...], unit[0 : lookup.shape[0], :])
        tables[:, index * 128 : index * 128 + 128] = block.astype(b16)
    tables[:, 256:] = table_topo[...]
    rows[0:1, :] = chain_ids[...].astype(f32)
    rows[1:2, :] = break_mask[...].astype(f32)
    position = lax.broadcasted_iota(jnp.int32, (1, 512), 1)
    rows[2:3, :] = jnp.where(position < res_counts[0], 0.0, -1e30)
    rows[3:8, :] = jnp.zeros((5, 512), f32)


def forward_inputs(
    time_embed,
    cath_class,
    cath_arch,
    cath_topo,
    res_counts,
    chain_ids,
    break_mask,
    w_qkv,
    w_out,
    w_gate,
    w_up,
    w_down,
    table_class,
    table_arch,
    table_topo,
    break_vec,
    pair_table,
    pair_proj,
):
    near = pl.BlockSpec(memory_space=pltpu.VMEM)
    flat = pl.BlockSpec(memory_space=pltpu.SMEM)
    count = 256 + table_topo.shape[0]
    shape = jax.ShapeDtypeStruct
    return pl.pallas_call(
        pack_kernel,
        name="pack",
        out_shape=[
            shape((48, 12288), b16),
            shape((16, 1, 128), f32),
            shape((16, 384), b16),
            shape((48, count), b16),
            shape((8, 512), f32),
        ],
        in_specs=[near] + [flat] * 4 + [near] * 13,
        out_specs=[near] * 5,
    )(
        time_embed,
        cath_class,
        cath_arch,
        cath_topo,
        res_counts,
        chain_ids,
        break_mask,
        w_qkv,
        w_out,
        w_gate,
        w_up,
        w_down.T,
        table_class,
        table_arch,
        table_topo.T,
        break_vec[None, :],
        pair_table.T,
        pair_proj,
    )


def unpack_kernel(
    summed,
    ada_in,
    tables,
    pair_in,
    proj_in,
    break_in,
    grad_ada,
    grad_qkv,
    grad_out,
    grad_gate,
    grad_up,
    grad_down,
    grad_class,
    grad_arch,
    grad_topo,
    grad_break,
    grad_pair,
    grad_proj,
):
    grad_ada[...] = ada_in[...]
    grad_qkv[...] = summed[:, 0:2304]
    grad_out[...] = summed[:, 2304:3072]
    grad_gate[...] = summed[:, 3072:6144]
    grad_up[...] = summed[:, 6144:9216]
    grad_down[...] = summed[:, 9216:12288]
    grad_class[...] = tables[:, 0:128].T[0 : grad_class.shape[0], :]
    grad_arch[...] = tables[:, 128:256].T[0 : grad_arch.shape[0], :]
    grad_topo[...] = tables[:, 256:]
    shard = lax.axis_index("fsdp") * 48
    total = jnp.zeros((1, 48), f32)
    for owner in range(16):
        row, column = divmod(owner * 48, 128)
        width = min(48, 128 - column)
        piece = break_in[row : row + 1, column : column + width]
        if width < 48:
            piece = jnp.concatenate([piece, break_in[row + 1 : row + 2, 0 : 48 - width]], axis=1)
        total = jnp.where(shard == owner * 48, piece, total)
    grad_break[...] = total
    grad_pair[...] = pair_in[...]
    grad_proj[...] = proj_in[:, 0:12]


def run_unpack(summed, ada, tables, pair, proj, breaks, sizes):
    near = pl.BlockSpec(memory_space=pltpu.VMEM)
    shape = jax.ShapeDtypeStruct
    outs = [
        (48, 4608),
        (48, 2304),
        (48, 768),
        (48, 3072),
        (48, 3072),
        (48, 3072),
        (sizes[0], 48),
        (sizes[1], 48),
        (48, sizes[2]),
        (1, 48),
        (16, 128),
        (16, 12),
    ]
    return pl.pallas_call(
        unpack_kernel,
        name="unpack",
        out_shape=[shape(one, f32) for one in outs],
        in_specs=[near] * 6,
        out_specs=[near] * 12,
    )(summed, ada, tables, pair, proj, breaks)


def fast_shards(
    tokens,
    cotangent,
    time_embed,
    cath_class,
    cath_arch,
    cath_topo,
    res_counts,
    chain_ids,
    break_mask,
    w_ada,
    w_qkv,
    w_out,
    w_gate,
    w_up,
    w_down,
    table_class,
    table_arch,
    table_topo,
    break_vec,
    pair_table,
    pair_proj,
):
    packed, first_note, pair_note, tables, rows = forward_inputs(
        time_embed,
        cath_class,
        cath_arch,
        cath_topo,
        res_counts,
        chain_ids,
        break_mask,
        w_qkv,
        w_out,
        w_gate,
        w_up,
        w_down,
        table_class,
        table_arch,
        table_topo,
        break_vec,
        pair_table,
        pair_proj,
    )
    output, *saved = run_forward(
        packed, tokens[0], cotangent[0], first_note, pair_note, w_ada, tables, rows
    )
    d_tokens, summed, grad_ada, grad_tables, grad_pair, grad_proj, grad_break = run_backward(
        saved, tokens[0], cotangent[0], w_ada, rows, tables.shape[1]
    )
    sizes = (table_class.shape[0], table_arch.shape[0], table_topo.shape[0])
    grads = run_unpack(summed, grad_ada, grad_tables, grad_pair, grad_proj, grad_break, sizes)
    return (
        output[None],
        d_tokens[None],
        *grads[:5],
        grads[5].T,
        grads[6],
        grads[7],
        grads[8].T,
        grads[9][0],
        grads[10].T,
        grads[11],
    )


def solution(mesh):
    in_specs = (
        P(("dp", "fsdp"), None, None),
        P(("dp", "fsdp"), None, None),
        P(("dp", "fsdp"), None),
        P(("dp", "fsdp")),
        P(("dp", "fsdp")),
        P(("dp", "fsdp")),
        P(("dp", "fsdp")),
        P(("dp", "fsdp"), None),
        P(("dp", "fsdp"), None),
        P("fsdp", None),
        P("fsdp", None),
        P("fsdp", None),
        P("fsdp", None),
        P("fsdp", None),
        P(None, "fsdp"),
        P(None, "fsdp"),
        P(None, "fsdp"),
        P(None, "fsdp"),
        P("fsdp"),
        P(None, "fsdp"),
        P("fsdp", None),
    )
    out_specs = (
        P(("dp", "fsdp"), None, None),
        P(("dp", "fsdp"), None, None),
        P("fsdp", None),
        P("fsdp", None),
        P("fsdp", None),
        P("fsdp", None),
        P("fsdp", None),
        P(None, "fsdp"),
        P(None, "fsdp"),
        P(None, "fsdp"),
        P(None, "fsdp"),
        P("fsdp"),
        P(None, "fsdp"),
        P("fsdp", None),
    )
    sizes = dict(mesh.shape)
    body = fast_shards if (sizes["dp"], sizes["fsdp"]) == (2, 16) else shards
    return jax.shard_map(body, mesh=mesh, in_specs=in_specs, out_specs=out_specs, check_vma=False)
```

profile of v0, /device:TPU:0, one launch (start us, length us, event | category | flops | bytes accessed | tf_op | source)
XLA Modules:
  0.0 241.0 jit_solution(8236479980914214349)
XLA Ops:
  3.2 2.6 %pack.1 = (bf16[48,12288]{1,0:T(8,128)(2,1)}, f32[16,1,128]{2,1,0:T(1,128)}, bf16[16,384]{1,0:T(8,128)(2,1)}, bf16[48,1728]{1,0:T(8,128)(2,1)}, f32[8,512]{1,0:T(8,128)}) custom-call(bf16[1,768]{1,0:T(2,128)(2,1)} %time_embed.1, s32[1]{0:T(128)S(6)} %copy.37.cath_class, s32[1]{0:T(128)S(6)} %copy.38.cath_arch, s32[1]{0:T(128)S(6)} %copy.39.cath_topo, ...), custom_call_target="tpu_custom_call" | custom-call | tf_op jit(solution)/shard_map/pack/pallas_call | solution.py:2065
  5.9 104.0 %forward.1 = (bf16[512,768]{1,0:T(8,128)(2,1)}, bf16[8,2,48,12288]{3,2,1,0:T(8,128)(2,1)}, bf16[512,768]{1,0:T(8,128)(2,1)}, bf16[512,2304]{1,0:T(8,128)(2,1)}, ...) custom-call(bf16[48,12288]{1,0:T(8,128)(2,1)} %get-tuple-element.55., ...), custom_call_target="tpu_custom_call" | custom-call | tf_op jit(solution)/shard_map/forward/pallas_call | solution.py:1108
  109.8 124.3 %backward.1 = (bf16[512,768]{1,0:T(8,128)(2,1)}, f32[48,12288]{1,0:T(8,128)}, f32[48,4608]{1,0:T(8,128)}, f32[48,1728]{1,0:T(8,128)}, f32[16,128]{1,0:T(8,128)}, /*index=5*/f32[16,128]{1,0:T(8,128)}, f32[8,128]{1,0:T(8,128)}) custom-call(bf16[8,2,48,12288]{3,2,1,0:T(8,128)(2,1)} %get-tuple-element.61.held, ...), custom_call_target="tpu_custom_call" | custom-call | tf_op jit(solution)/shard_map/backward/pallas_call | solution.py:1943
  234.1 0.0 copy-start
  234.2 0.0 copy-start.1
  234.2 5.0 %unpack.1 = (f32[48,4608]{1,0:T(8,128)}, f32[48,2304]{1,0:T(8,128)}, f32[48,768]{1,0:T(8,128)}, f32[48,3072]{1,0:T(8,128)}, f32[48,3072]{1,0:T(8,128)}, /*index=...) custom-call(f32[48,12288]{1,0:T(8,128)} %get-tuple-element.78.summed, ...), custom_call_target="tpu_custom_call" | custom-call | tf_op jit(solution)/shard_map/unpack/pallas_call | solution.py:2159
  239.2 0.0 copy-done
  239.2 0.9 copy.41
  240.1 0.0 copy-done.1
  240.1 0.9 copy.42
Async XLA Ops:
  234.1 5.1 %copy-start = (bf16[512,768]{1,0:T(8,128)(2,1)S(1)}, bf16[512,768]{1,0:T(8,128)(2,1)}, u32[]{:S(2)}) copy-start(bf16[512,768]{1,0:T(8,128)(2,1)} %get-tuple-element.60) | copy-start | bytes 2359300
  234.2 5.9 %copy-start.1 = (bf16[512,768]{1,0:T(8,128)(2,1)S(1)}, bf16[512,768]{1,0:T(8,128)(2,1)}, u32[]{:S(2)}) copy-start(bf16[512,768]{1,0:T(8,128)(2,1)} %get-tuple-element.77) | copy-start | bytes 2359300
where the time goes:
time: 241 us
  Pallas kernels  236 us (98%)
  between operations  3.27 us (1%)
    pallas_call x1, Pallas kernels, run_backward(): pl.pallas_call(backward_kernel, name='backward', out_shape=[one for one,...  124 us
    pallas_call x1, Pallas kernels, run_forward(): pl.pallas_call(forward_kernel, name='forward', out_shape=[one for one, _...  104 us
    pallas_call x1, Pallas kernels, run_unpack(): pl.pallas_call(unpack_kernel, name='unpack', out_shape=[shape(one, f32) f...  5.03 us

commit v1 on v0

--- a/solution.py
+++ b/solution.py
@@ -461,7 +461,7 @@
 gather_stride = 2
 scatter_stride = 2
 grad_buffers = 3
-plan = (1, 1, 1, 1, 1, 1, 1, 1, 1, 1, 5)
+plan = (1, 1, 1, 1, 1, 1, 1, 1, 1, 1, 4)
 ahead_plan = (2, 2, 2, 2, 2)
 
 
@@ -1515,11 +1515,15 @@
         )
         scatter.core_start(turn, part)
 
-    def merge(turn):
+    def merge_sides(turn):
         scatter.core_add(turn, 0)
         scatter.core_add(turn, 3)
         scatter.side(turn, 0).start()
         scatter.side(turn, 1).start()
+
+    def merge(turn, sides=True):
+        if sides:
+            merge_sides(turn)
         scatter.core_add(turn, 1)
         scatter.core_add(turn, 2)
         scatter.begin(turn, False)
@@ -1718,6 +1722,7 @@
     put(3, 0, hidden[...], gate[:, 0:768])
     scatter.step(plan[7])
     put(3, 1, hidden[...], gate[:, 768:1536])
+    merge_sides(3)
     put(3, 2, hidden[...], gate[:, 1536:2304])
     for part in range(3):
         product = dot_nt(gate[:, part * 768 : part * 768 + 768], piece(13 + part))
@@ -1726,7 +1731,7 @@
         else:
             d_hid[...] += product
         if part == 0:
-            merge(3)
+            merge(3, False)
             scatter.begin(3, True, plan[10])
         scatter.step(plan[8])
     tokens_load.wait()

time: 241 us -> 239 us (level)
  no operation moved by 1% of the time
where the time goes in v1:
time: 239 us
  Pallas kernels  234 us (98%)
  between operations  3.27 us (1%)
    pallas_call x1, Pallas kernels, run_backward(): pl.pallas_call(backward_kernel, name='backward', out_shape=[one for one,...  123 us
    pallas_call x1, Pallas kernels, run_forward(): pl.pallas_call(forward_kernel, name='forward', out_shape=[one for one, _...  104 us
    pallas_call x1, Pallas kernels, run_unpack(): pl.pallas_call(unpack_kernel, name='unpack', out_shape=[shape(one, f32) f...  5.03 us

profile of v1, /device:TPU:0, one launch (start us, length us, event | category | flops | bytes accessed | tf_op | source)
XLA Modules:
  0.0 239.2 jit_solution(4114554668880456506)
XLA Ops:
  3.2 2.6 %pack.1 = (bf16[48,12288]{1,0:T(8,128)(2,1)}, f32[16,1,128]{2,1,0:T(1,128)}, bf16[16,384]{1,0:T(8,128)(2,1)}, bf16[48,1728]{1,0:T(8,128)(2,1)}, f32[8,512]{1,0:T(8,128)}) custom-call(bf16[1,768]{1,0:T(2,128)(2,1)} %time_embed.1, s32[1]{0:T(128)S(6)} %copy.37.cath_class, s32[1]{0:T(128)S(6)} %copy.38.cath_arch, s32[1]{0:T(128)S(6)} %copy.39.cath_topo, ...), custom_call_target="tpu_custom_call" | custom-call | tf_op jit(solution)/shard_map/pack/pallas_call | solution.py:2070
  5.9 104.0 %forward.1 = (bf16[512,768]{1,0:T(8,128)(2,1)}, bf16[8,2,48,12288]{3,2,1,0:T(8,128)(2,1)}, bf16[512,768]{1,0:T(8,128)(2,1)}, bf16[512,2304]{1,0:T(8,128)(2,1)}, ...) custom-call(bf16[48,12288]{1,0:T(8,128)(2,1)} %get-tuple-element.55., ...), custom_call_target="tpu_custom_call" | custom-call | tf_op jit(solution)/shard_map/forward/pallas_call | solution.py:1108
  109.8 122.5 %backward.1 = (bf16[512,768]{1,0:T(8,128)(2,1)}, f32[48,12288]{1,0:T(8,128)}, f32[48,4608]{1,0:T(8,128)}, f32[48,1728]{1,0:T(8,128)}, f32[16,128]{1,0:T(8,128)}, /*index=5*/f32[16,128]{1,0:T(8,128)}, f32[8,128]{1,0:T(8,128)}) custom-call(bf16[8,2,48,12288]{3,2,1,0:T(8,128)(2,1)} %get-tuple-element.61.held, ...), custom_call_target="tpu_custom_call" | custom-call | tf_op jit(solution)/shard_map/backward/pallas_call | solution.py:1948
  232.4 0.0 copy-start
  232.4 0.0 copy-start.1
  232.4 5.0 %unpack.1 = (f32[48,4608]{1,0:T(8,128)}, f32[48,2304]{1,0:T(8,128)}, f32[48,768]{1,0:T(8,128)}, f32[48,3072]{1,0:T(8,128)}, f32[48,3072]{1,0:T(8,128)}, /*index=...) custom-call(f32[48,12288]{1,0:T(8,128)} %get-tuple-element.78.summed, ...), custom_call_target="tpu_custom_call" | custom-call | tf_op jit(solution)/shard_map/unpack/pallas_call | solution.py:2164
  237.4 0.0 copy-done
  237.4 0.9 copy.41
  238.3 0.0 copy-done.1
  238.3 0.9 copy.42
Async XLA Ops:
  232.4 5.1 %copy-start = (bf16[512,768]{1,0:T(8,128)(2,1)S(1)}, bf16[512,768]{1,0:T(8,128)(2,1)}, u32[]{:S(2)}) copy-start(bf16[512,768]{1,0:T(8,128)(2,1)} %get-tuple-element.60) | copy-start | bytes 2359300
  232.4 5.9 %copy-start.1 = (bf16[512,768]{1,0:T(8,128)(2,1)S(1)}, bf16[512,768]{1,0:T(8,128)(2,1)}, u32[]{:S(2)}) copy-start(bf16[512,768]{1,0:T(8,128)(2,1)} %get-tuple-element.77) | copy-start | bytes 2359300
